TPU v7x, 32 devices: a whole 2x2x4 slice. The times are simulated.
32 devices in a mesh: group: 2 (over x), seq: 16 (over z, y, core).
Axes of the slice: x: 2, y: 2, z: 4, core: 2. Of those that a mesh axis runs over, the one named last changes fastest.
Arguments:
- x_rows: bfloat16 [32, 8192], P('group', 'seq'), parts along dimension 0, may hold values from -0.59765625 to 0.59765625
- attn_gain: bfloat16 [8192], replicated, may hold values from 0.5 to 1.5
- q_weight: bfloat16 [8192, 8192], P(None, 'seq'), may hold values from -0.0625 to 0.0625
- o_weight: bfloat16 [8192, 8192], P('seq'), may hold values from -0.0625 to 0.0625
- mlp_gain: bfloat16 [8192], replicated, may hold values from 0.5 to 1.5
- gate_weight: bfloat16 [8192, 14336], P(None, 'seq'), may hold values from -0.0625 to 0.0625
- up_weight: bfloat16 [8192, 14336], P(None, 'seq'), may hold values from -0.0625 to 0.0625
- down_weight: bfloat16 [14336, 8192], P('seq'), may hold values from -0.046875 to 0.046875
- kv_cache: bfloat16 [2, 4096, 1024], P(None, ('group', 'seq')), parts along dimension 1, may hold values from -250 to 250, as said below
- block_mask: int32 [32, 8, 16], P('group', None, 'seq'), parts along dimension 0, may hold values from 0 to 1, as said below
Outputs:
- y_rows: bfloat16 [32, 8192], P('group', 'seq'), parts along dimension 0
There are 2 independent parts, one for each index of `group`. A program takes and returns all parts, laid end to end along the dimension named above; an argument that names none is the same for every part. Nothing has to cross between parts.
Inputs may be any that keep to these rules, and one draw needn't show every extreme that they name: `kv_cache`: document keys and values; they differ from document to document. `block_mask`: 1 where the row may attend to that block of 128 document tokens for that key-value head, else 0; the document's last block is 1 for every row and key-value head.
All inputs are finite; a program needn't handle non-finite values.
Results may differ from a plain program's by a relative error of at most 0.013.
The roundings to bfloat16 on the way count: a program that leaves them out, or rounds other values in their place, can miss the bound.
Values may be sent and summed in bfloat16 or wider, within the bound.
A program may use at most 192 MiB of HBM per device.

v0:
```python
import functools

import jax
import jax.numpy as jnp
from jax import lax
from jax.experimental import pallas as pl
from jax.experimental.pallas import tpu as pltpu
from jax.sharding import PartitionSpec as P

HEADS = 64
KV_HEADS = 8
HEAD_DIM = 128
BLOCK = 128


eps = 1e-05
floor_score = -1e30


def combined_all(x, axis, combine):
    everything = jax.tree.map(lambda part: lax.all_gather(part, axis), x)
    initial = jax.tree.map(lambda part: part[0], everything)

    def turn(k, so_far):
        return combine(so_far, jax.tree.map(lambda part: part[k], everything))

    return lax.fori_loop(1, lax.axis_size(axis), turn, initial)


def rms_norm(values, gain):
    wide = values.astype(jnp.float32)
    inverse = lax.rsqrt(jnp.mean(wide * wide, axis=-1, keepdims=True) + eps)
    return (wide * inverse * gain.astype(jnp.float32)).astype(jnp.bfloat16)


def combine_states(first, second):
    top_a, total_a, accum_a = first
    top_b, total_b, accum_b = second
    top = jnp.maximum(top_a, top_b)
    factor_a = jnp.exp(top_a - top)
    factor_b = jnp.exp(top_b - top)
    return (
        top,
        total_a * factor_a + total_b * factor_b,
        accum_a * factor_a[..., None] + accum_b * factor_b[..., None],
    )


def local(
    x_rows,
    attn_gain,
    q_weight,
    o_weight,
    mlp_gain,
    gate_weight,
    up_weight,
    down_weight,
    kv_cache,
    block_mask,
):
    rows = x_rows.shape[0]
    group = HEADS // KV_HEADS
    key_len = kv_cache.shape[1]
    spans = key_len // BLOCK
    scale = 1.0 / HEAD_DIM**0.5
    whole = lax.all_gather(x_rows, "seq", axis=1, tiled=True)
    normed = rms_norm(whole, attn_gain)
    query_part = jnp.dot(normed, q_weight, preferred_element_type=jnp.float32).astype(jnp.bfloat16)
    queries = lax.all_gather(query_part, "seq", axis=1, tiled=True)
    doc_keys = kv_cache[0]
    doc_values = kv_cache[1]

    def one_group(index):
        query_group = lax.dynamic_slice_in_dim(
            queries, index * (group * HEAD_DIM), group * HEAD_DIM, 1
        ).reshape(rows, group, HEAD_DIM)
        key_group = lax.dynamic_slice_in_dim(doc_keys, index * HEAD_DIM, HEAD_DIM, 1)
        value_group = lax.dynamic_slice_in_dim(doc_values, index * HEAD_DIM, HEAD_DIM, 1)
        mask_group = lax.dynamic_slice_in_dim(block_mask, index, 1, 1)[:, 0, :]
        scores = (
            jnp.einsum("rhd,kd->rhk", query_group, key_group, preferred_element_type=jnp.float32)
            * scale
        )
        scores = scores.reshape(rows, group, spans, BLOCK)
        live = (mask_group == 1)[:, None, :, None]
        masked = jnp.where(live, scores, floor_score)
        local_top = jnp.max(masked, axis=(2, 3))
        weights = jnp.where(live, jnp.exp(masked - local_top[..., None, None]), 0.0)
        local_total = jnp.sum(weights, axis=(2, 3))
        rounded = weights.astype(jnp.bfloat16).reshape(rows, group, key_len)
        local_accum = jnp.einsum(
            "rhk,kd->rhd", rounded, value_group, preferred_element_type=jnp.float32
        )
        return (local_top, local_total, local_accum)

    tops, totals, accums = lax.map(one_group, jnp.arange(KV_HEADS, dtype=jnp.int32))
    local_top = jnp.moveaxis(tops, 0, 1)
    local_total = jnp.moveaxis(totals, 0, 1)
    local_accum = jnp.moveaxis(accums, 0, 1)
    columns = q_weight.shape[1]
    col_start = lax.axis_index("seq") * columns
    top, total, accum = combined_all((local_top, local_total, local_accum), "seq", combine_states)
    attended = accum / total[..., None]
    attended = attended.reshape(rows, HEADS * HEAD_DIM).astype(jnp.bfloat16)
    attn_cols = lax.dynamic_slice_in_dim(attended, col_start, columns, 1)
    weight_cols = o_weight
    attn_out = lax.psum_scatter(
        lax.dot_general(
            weight_cols, attn_cols, (((0,), (1,)), ((), ())), preferred_element_type=jnp.float32
        ),
        "seq",
        scatter_dimension=0,
        tiled=True,
    )
    stream = (x_rows.astype(jnp.float32) + attn_out.T).astype(jnp.bfloat16)
    stream_whole = lax.all_gather(stream, "seq", axis=1, tiled=True)
    normed_two = rms_norm(stream_whole, mlp_gain)
    gate = jnp.dot(normed_two, gate_weight, preferred_element_type=jnp.float32)
    upward = jnp.dot(normed_two, up_weight, preferred_element_type=jnp.float32)
    hidden = (jax.nn.silu(gate) * upward).astype(jnp.bfloat16)
    weight_cols = down_weight
    down_out = lax.psum_scatter(
        lax.dot_general(
            weight_cols, hidden, (((0,), (1,)), ((), ())), preferred_element_type=jnp.float32
        ),
        "seq",
        scatter_dimension=0,
        tiled=True,
    )
    return (stream.astype(jnp.float32) + down_out.T).astype(jnp.bfloat16)


FAR_FIRST = (4, 3, 5, 2, 6, 1, 7)
SCALE = 1.0 / HEAD_DIM**0.5


def layer_kernel(
    x_ref,
    attn_gain,
    q_hbm,
    o_hbm,
    mlp_gain,
    gate_hbm,
    up_hbm,
    down_hbm,
    kv_hbm,
    mask_ref,
    y_ref,
    q_w,
    o_w,
    gate_w,
    up_w,
    down_w,
    x_all,
    s_all,
    normed,
    stream_ref,
    kv_all,
    mask_out,
    mask_all,
    scores,
    part_one,
    got_one,
    part_two,
    got_two,
    own_ref,
    w_sem,
    kv_own_sem,
    x_send,
    x_recv,
    x_pass,
    s_send,
    s_recv,
    s_pass,
    kv_send,
    kv_recv,
    kv_pass,
    m_send,
    m_recv,
    m_pass,
    one_send,
    one_recv,
    two_send,
    two_recv,
):
    devices, rows, cols = x_all.shape
    chips = devices // 2
    group = cols // HEAD_DIM
    me = lax.axis_index("seq")
    chip = me // 2
    core = me % 2
    partner = chip * 2 + 1 - core

    def fetch(k, src, dst):
        return pltpu.make_async_copy(src, dst, w_sem.at[k])

    def remote(src, dst, send, recv, device):
        return pltpu.make_async_remote_copy(
            src_ref=src,
            dst_ref=dst,
            send_sem=send,
            recv_sem=recv,
            device_id={"seq": device},
            device_id_type=pl.DeviceIdType.MESH,
        )

    def chip_at(off):
        return (chip + off) % chips

    def gather_start(src, dst, send, recv):
        for off in FAR_FIRST:
            remote(src, dst.at[me], send.at[off], recv.at[me], chip_at(off) * 2 + core).start()
        remote(src, dst.at[me], send.at[0], recv.at[me], partner).start()

    def gather_pass(dst, send, recv, hand):
        for off in reversed(FAR_FIRST):
            other = chip_at(off) * 2 + core
            remote(dst.at[other], dst.at[other], send.at[off], recv.at[other], partner).wait_recv()
            remote(dst.at[other], dst.at[other], hand.at[off], recv.at[other], partner).start()

    def gather_finish(dst, send, recv):
        for off in range(chips):
            other = chip_at(off) * 2 + 1 - core
            remote(dst.at[other], dst.at[other], send.at[0], recv.at[other], partner).wait_recv()

    def gather_drain(src, dst, send, recv, hand):
        for off in range(chips):
            remote(src, dst.at[me], send.at[off], recv.at[me], partner).wait_send()
        for off in FAR_FIRST:
            remote(src, dst.at[me], hand.at[off], recv.at[me], partner).wait_send()

    fetch_q = fetch(0, q_hbm, q_w)
    fetch_o = fetch(1, o_hbm, o_w)
    fetch_gate = fetch(2, gate_hbm, gate_w)
    fetch_up = fetch(3, up_hbm, up_w)
    fetch_down = fetch(4, down_hbm, down_w)

    barrier = pltpu.get_barrier_semaphore()
    for off in range(1, devices):
        pl.semaphore_signal(
            barrier,
            inc=1,
            device_id={"seq": (me + off) % devices},
            device_id_type=pl.DeviceIdType.MESH,
        )
    fetch_q.start()
    own_kv = pltpu.make_async_copy(
        kv_hbm.at[:, :, pl.ds(pl.multiple_of(chip * HEAD_DIM, HEAD_DIM), HEAD_DIM)],
        kv_all.at[me],
        kv_own_sem,
    )
    own_kv.start()
    fetch_o.start()
    for g in range(KV_HEADS):
        mask_out[g] = jnp.broadcast_to(
            mask_ref[:, g : g + 1].astype(jnp.float32), (rows, HEAD_DIM)
        )
    mask_all[me] = mask_out[chip]
    x_all[me] = x_ref[...]
    pl.semaphore_wait(barrier, devices - 1)

    gather_start(x_ref, x_all, x_send, x_recv)

    def kv_of(where):
        return kv_hbm.at[:, :, pl.ds(pl.multiple_of(where * HEAD_DIM, HEAD_DIM), HEAD_DIM)]

    for off in FAR_FIRST:
        there = chip_at(off)
        to = there * 2 + core
        remote(kv_of(there), kv_all.at[me], kv_send.at[off], kv_recv.at[me], to).start()
        remote(mask_out.at[there], mask_all.at[me], m_send.at[off], m_recv.at[me], to).start()
    remote(kv_of(chip), kv_all.at[me], kv_send.at[0], kv_recv.at[me], partner).start()
    remote(mask_out.at[chip], mask_all.at[me], m_send.at[0], m_recv.at[me], partner).start()
    fetch_gate.start()
    fetch_up.start()
    fetch_down.start()

    def norm(values, gain):
        squares = jnp.zeros((rows, cols), jnp.float32)
        for i in range(devices):
            wide = values[i].astype(jnp.float32)
            squares = squares + wide * wide
        mean = jnp.sum(squares, axis=-1, keepdims=True) * (1.0 / (devices * cols))
        inverse = lax.rsqrt(mean + eps)
        for i in range(devices):
            part_gain = gain[i * cols : (i + 1) * cols].astype(jnp.float32).reshape(1, cols)
            normed[i] = (values[i].astype(jnp.float32) * inverse * part_gain).astype(jnp.bfloat16)

    gather_pass(x_all, x_send, x_recv, x_pass)
    gather_finish(x_all, x_send, x_recv)
    norm(x_all, attn_gain)
    fetch_q.wait()
    step = 4

    def q_step(t, total):
        for u in range(step):
            i = t * step + u
            total = total + jnp.dot(
                normed[i],
                q_w[pl.ds(pl.multiple_of(i * cols, cols), cols), :],
                preferred_element_type=jnp.float32,
            )
        return total

    queries = lax.fori_loop(
        0, devices // step, q_step, jnp.zeros((rows, cols), jnp.float32)
    ).astype(jnp.bfloat16)
    query = jnp.concatenate(
        [queries[:, h * HEAD_DIM : (h + 1) * HEAD_DIM] for h in range(group)], axis=0
    )

    gather_pass(kv_all, kv_send, kv_recv, kv_pass)
    gather_pass(mask_all, m_send, m_recv, m_pass)
    own_kv.wait()
    gather_finish(kv_all, kv_send, kv_recv)
    gather_finish(mask_all, m_send, m_recv)

    def live_at(c):
        return jnp.concatenate([mask_all[c]] * group, axis=0) > 0.5

    tops = []
    for c in range(devices):
        score = (
            lax.dot_general(
                query,
                kv_all[c, 0],
                (((1,), (1,)), ((), ())),
                preferred_element_type=jnp.float32,
            )
            * SCALE
        )
        masked = jnp.where(live_at(c), score, floor_score)
        scores[c] = masked
        tops.append(jnp.max(masked, axis=-1, keepdims=True))
    top = functools.reduce(jnp.maximum, tops)
    total = jnp.zeros((group * rows, 1), jnp.float32)
    accum = jnp.zeros((group * rows, HEAD_DIM), jnp.float32)
    for c in range(devices):
        weight = jnp.where(live_at(c), jnp.exp(scores[c] - tops[c]), 0.0)
        factor = jnp.exp(tops[c] - top)
        total = total + factor * jnp.sum(weight, axis=-1, keepdims=True)
        accum = accum + factor * jnp.dot(
            weight.astype(jnp.bfloat16), kv_all[c, 1], preferred_element_type=jnp.float32
        )
    ratio = accum / total
    attended = jnp.concatenate(
        [ratio[h * rows : (h + 1) * rows] for h in range(group)], axis=1
    ).astype(jnp.bfloat16)

    def scatter(values, weight, part, got, send, recv):
        def target(s):
            off = devices // 2 + ((s + 1) // 2) * (1 - 2 * (s % 2))
            return (me + off) % devices

        def post(s):
            to = target(s)
            remote(part.at[to], got.at[me], send.at[s], recv.at[me], to).start()

        def product(s):
            to = target(s)
            return jnp.dot(
                values,
                weight[:, pl.ds(pl.multiple_of(to * cols, cols), cols)],
                preferred_element_type=jnp.float32,
            )

        def turn(t, _):
            first = product(2 * t)
            second = product(2 * t + 1)
            part[target(2 * t)] = first.astype(part.dtype)
            part[target(2 * t + 1)] = second.astype(part.dtype)
            own_ref[...] = second

            @pl.when(t > 0)
            def _():
                post(2 * t - 2)
                post(2 * t - 1)

            return 0

        lax.fori_loop(0, devices // 2, turn, 0)
        post(devices - 2)

        def add(s, total):
            other = target(devices - 2 - s)
            remote(part.at[other], got.at[other], send.at[s], recv.at[other], other).wait_recv()
            return total + got[other].astype(jnp.float32)

        return lax.fori_loop(0, devices - 1, add, own_ref[...])

    def scatter_drain(part, got, send, recv):
        for s in range(devices - 1):
            remote(part.at[0], got.at[me], send.at[s], recv.at[me], partner).wait_send()

    fetch_o.wait()
    attn_out = scatter(attended, o_w, part_one, got_one, one_send, one_recv)
    stream = (x_ref[...].astype(jnp.float32) + attn_out).astype(jnp.bfloat16)
    stream_ref[...] = stream
    s_all[me] = stream
    gather_start(stream_ref, s_all, s_send, s_recv)
    gather_pass(s_all, s_send, s_recv, s_pass)
    gather_finish(s_all, s_send, s_recv)
    norm(s_all, mlp_gain)
    fetch_gate.wait()
    fetch_up.wait()
    wide = gate_w.shape[1]

    def ff_step(t, sums):
        gate, upward = sums
        for u in range(2):
            i = t * 2 + u
            at = pl.ds(pl.multiple_of(i * cols, cols), cols)
            gate = gate + jnp.dot(normed[i], gate_w[at, :], preferred_element_type=jnp.float32)
            upward = upward + jnp.dot(normed[i], up_w[at, :], preferred_element_type=jnp.float32)
        return gate, upward

    zeros = jnp.zeros((rows, wide), jnp.float32)
    gate, upward = lax.fori_loop(0, devices // 2, ff_step, (zeros, zeros))
    hidden = (gate / (1.0 + jnp.exp(-gate)) * upward).astype(jnp.bfloat16)
    fetch_down.wait()
    down_out = scatter(hidden, down_w, part_two, got_two, two_send, two_recv)
    y_ref[...] = (stream_ref[...].astype(jnp.float32) + down_out).astype(jnp.bfloat16)

    gather_drain(x_ref, x_all, x_send, x_recv, x_pass)
    gather_drain(kv_of(chip), kv_all, kv_send, kv_recv, kv_pass)
    gather_drain(mask_out.at[0], mask_all, m_send, m_recv, m_pass)
    gather_drain(stream_ref, s_all, s_send, s_recv, s_pass)
    scatter_drain(part_one, got_one, one_send, one_recv)
    scatter_drain(part_two, got_two, two_send, two_recv)


def layer(
    x_rows,
    attn_gain,
    q_weight,
    o_weight,
    mlp_gain,
    gate_weight,
    up_weight,
    down_weight,
    kv_cache,
    block_mask,
):
    rows, cols = x_rows.shape
    devices = lax.axis_size("seq")
    chips = devices // 2
    wide = gate_weight.shape[1]
    dma = pltpu.SemaphoreType.DMA
    held = pl.BlockSpec(memory_space=pltpu.VMEM)
    left = pl.BlockSpec(memory_space=pl.ANY)
    exchange = pltpu.VMEM((devices, rows, cols), jnp.bfloat16)
    return pl.pallas_call(
        layer_kernel,
        name="layer",
        out_shape=jax.ShapeDtypeStruct((rows, cols), jnp.bfloat16),
        in_specs=[held, held, left, left, held, left, left, left, left, held],
        out_specs=held,
        scratch_shapes=[
            pltpu.VMEM(q_weight.shape, jnp.bfloat16),
            pltpu.VMEM(o_weight.shape, jnp.bfloat16),
            pltpu.VMEM(gate_weight.shape, jnp.bfloat16),
            pltpu.VMEM(up_weight.shape, jnp.bfloat16),
            pltpu.VMEM(down_weight.shape, jnp.bfloat16),
            exchange,
            exchange,
            exchange,
            pltpu.VMEM((rows, cols), jnp.bfloat16),
            pltpu.VMEM((devices, 2, BLOCK, HEAD_DIM), jnp.bfloat16),
            pltpu.VMEM((KV_HEADS, rows, HEAD_DIM), jnp.float32),
            pltpu.VMEM((devices, rows, HEAD_DIM), jnp.float32),
            pltpu.VMEM((devices, rows * cols // HEAD_DIM, BLOCK), jnp.float32),
            exchange,
            exchange,
            exchange,
            exchange,
            pltpu.VMEM((rows, cols), jnp.float32),
            dma((5,)),
            dma(()),
            *([dma((chips,)), dma((devices,)), dma((chips,))] * 4),
            *([dma((devices,))] * 4),
        ],
        compiler_params=pltpu.CompilerParams(
            collective_id=0, has_side_effects=True, vmem_limit_bytes=67043328
        ),
    )(
        x_rows,
        attn_gain,
        q_weight,
        o_weight,
        mlp_gain,
        gate_weight,
        up_weight,
        down_weight,
        kv_cache,
        block_mask[:, :, 0],
    )


def solution(mesh):
    fused = mesh.shape["seq"] == 2 * KV_HEADS
    return jax.shard_map(
        layer if fused else local,
        mesh=mesh,
        in_specs=(
            P("group", "seq"),
            P(),
            P(None, "seq"),
            P("seq", None),
            P(),
            P(None, "seq"),
            P(None, "seq"),
            P("seq", None),
            P(None, ("group", "seq"), None),
            P("group", None, "seq"),
        ),
        out_specs=P("group", "seq"),
        check_vma=False,
    )
```

profile of v0, /device:TPU:0, one launch (start us, length us, event | category | flops | bytes accessed | tf_op | source)
XLA Modules:
  0.0 57.6 jit_solution(1115243820792359809)
XLA Ops:
  0.0 1.4 %copy.11.mask_ref = s32[16,8]{1,0:T(8,128)} copy(s32[16,8]{0,1:T(8,128)} %bitcast.1) | data formatting | bytes 1024 | tf_op jit(solution)/shard_map/squeeze | solution.py:495
  1.4 54.9 %layer.1 = bf16[16,512]{1,0:T(8,128)(2,1)} custom-call(bf16[16,512]{1,0:T(8,128)(2,1)} %x_ref.1, bf16[8192]{0:T(1024)(128)(2,1)} %attn_gain.1, bf16[8192,512]{1,0:T(8,128)(2,1)} %q_hbm.1, bf16[512,8192]{1,0:T(8,128)(2,1)} %o_hbm.1, bf16[8192]{0:T(1024)(128)(2,1)} %mlp_gain.1, bf16[8192,896]{1,0:T(8,128)(2,1)} %gate_hbm.1, bf16[8192,896]{1,0:T(8,128)(2,1)} %up_hbm.1, ...), custom_call_target="tpu_custom_call" | custom-call | tf_op jit(solution)/shard_map/layer/pallas_call | solution.py:452
  56.3 1.3 %copy.13 = bf16[16,512]{1,0:T(8,128)(2,1)} copy(bf16[16,512]{1,0:T(8,128)(2,1)} %layer.1) | data formatting | bytes 32768
where the time goes:
time: 58 us; the launch traced here: 57.6 us
  Pallas kernels  54.9 us (95%)
  local copies, waits for them, and re-layouts  2.68 us (5%)
    pallas_call x1, Pallas kernels, layer(): pl.pallas_call(layer_kernel, name='layer', out_shape=jax.ShapeDtypeStruct...  54.9 us
    squeeze x1, local copies, waits for them, and re-layouts, layer(): block_mask[:, :, 0]  1.35 us
    unnamed x1, local copies, waits for them, and re-layouts  1.32 us

commit v1 on v0

--- a/solution.py
+++ b/solution.py
@@ -159,6 +159,8 @@
     mask_out,
     mask_all,
     scores,
+    pair_out,
+    pair_in,
     part_one,
     got_one,
     part_two,
@@ -178,11 +180,9 @@
     m_send,
     m_recv,
     m_pass,
-    one_send,
-    one_recv,
-    two_send,
-    two_recv,
+    *scatter_sems,
 ):
+    one_sems, two_sems = scatter_sems[:4], scatter_sems[4:]
     devices, rows, cols = x_all.shape
     chips = devices // 2
     group = cols // HEAD_DIM
@@ -347,53 +347,86 @@
         [ratio[h * rows : (h + 1) * rows] for h in range(group)], axis=1
     ).astype(jnp.bfloat16)
 
-    def scatter(values, weight, part, got, send, recv):
-        def target(s):
-            off = devices // 2 + ((s + 1) // 2) * (1 - 2 * (s % 2))
-            return (me + off) % devices
-
-        def post(s):
-            to = target(s)
-            remote(part.at[to], got.at[me], send.at[s], recv.at[me], to).start()
-
-        def product(s):
-            to = target(s)
+    def scatter(values, weight, pair_out, pair_in, part, got, sems):
+        pair_send, pair_recv, send, recv = sems
+
+        def chip_of(s):
+            off = chips // 2 + ((s + 1) // 2) * (1 - 2 * (s % 2))
+            return chip_at(off)
+
+        def product(where, half):
+            to = where * 2 + half
             return jnp.dot(
                 values,
                 weight[:, pl.ds(pl.multiple_of(to * cols, cols), cols)],
                 preferred_element_type=jnp.float32,
             )
 
-        def turn(t, _):
-            first = product(2 * t)
-            second = product(2 * t + 1)
-            part[target(2 * t)] = first.astype(part.dtype)
-            part[target(2 * t + 1)] = second.astype(part.dtype)
-            own_ref[...] = second
+        def to_partner(s):
+            to = chip_of(s)
+            return remote(pair_out.at[to], pair_in.at[to], pair_send.at[s], pair_recv.at[to], partner)
+
+        def to_chip(s):
+            to = chip_of(s)
+            return remote(part.at[to], got.at[chip], send.at[s], recv.at[chip], to * 2 + core)
+
+        def pair_turn(t, _):
+            first = product(chip_of(2 * t), 1 - core)
+            second = product(chip_of(2 * t + 1), 1 - core)
+            pair_out[chip_of(2 * t)] = first
+            pair_out[chip_of(2 * t + 1)] = second
 
             @pl.when(t > 0)
             def _():
-                post(2 * t - 2)
-                post(2 * t - 1)
+                to_partner(2 * t - 2).start()
+                to_partner(2 * t - 1).start()
 
             return 0
 
-        lax.fori_loop(0, devices // 2, turn, 0)
-        post(devices - 2)
-
-        def add(s, total):
-            other = target(devices - 2 - s)
-            remote(part.at[other], got.at[other], send.at[s], recv.at[other], other).wait_recv()
-            return total + got[other].astype(jnp.float32)
-
-        return lax.fori_loop(0, devices - 1, add, own_ref[...])
-
-    def scatter_drain(part, got, send, recv):
-        for s in range(devices - 1):
-            remote(part.at[0], got.at[me], send.at[s], recv.at[me], partner).wait_send()
+        lax.fori_loop(0, chips // 2, pair_turn, 0)
+
+        def chip_turn(t, _):
+            one, two = chip_of(2 * t), chip_of(2 * t + 1)
+            first = product(one, core)
+            second = product(two, core)
+
+            @pl.when(t == 0)
+            def _():
+                to_partner(chips - 2).start()
+                to_partner(chips - 1).start()
+
+            to_partner(2 * t).wait_recv()
+            to_partner(2 * t + 1).wait_recv()
+            second = second + pair_in[two]
+            part[one] = (first + pair_in[one]).astype(part.dtype)
+            part[two] = second.astype(part.dtype)
+            own_ref[...] = second
+
+            @pl.when(t > 0)
+            def _():
+                to_chip(2 * t - 2).start()
+                to_chip(2 * t - 1).start()
+
+            return 0
+
+        lax.fori_loop(0, chips // 2, chip_turn, 0)
+        to_chip(chips - 2).start()
+        total = own_ref[...]
+        for off in reversed(FAR_FIRST):
+            other = chip_at(off)
+            remote(part.at[other], got.at[other], send.at[0], recv.at[other], partner).wait_recv()
+            total = total + got[other].astype(jnp.float32)
+        for s in range(chips):
+            to_partner(s).wait_send()
+        return total
+
+    def scatter_drain(part, got, sems):
+        _, _, send, recv = sems
+        for s in range(chips - 1):
+            remote(part.at[0], got.at[chip], send.at[s], recv.at[chip], partner).wait_send()
 
     fetch_o.wait()
-    attn_out = scatter(attended, o_w, part_one, got_one, one_send, one_recv)
+    attn_out = scatter(attended, o_w, pair_out, pair_in, part_one, got_one, one_sems)
     stream = (x_ref[...].astype(jnp.float32) + attn_out).astype(jnp.bfloat16)
     stream_ref[...] = stream
     s_all[me] = stream
@@ -418,15 +451,15 @@
     gate, upward = lax.fori_loop(0, devices // 2, ff_step, (zeros, zeros))
     hidden = (gate / (1.0 + jnp.exp(-gate)) * upward).astype(jnp.bfloat16)
     fetch_down.wait()
-    down_out = scatter(hidden, down_w, part_two, got_two, two_send, two_recv)
+    down_out = scatter(hidden, down_w, pair_out, pair_in, part_two, got_two, two_sems)
     y_ref[...] = (stream_ref[...].astype(jnp.float32) + down_out).astype(jnp.bfloat16)
 
     gather_drain(x_ref, x_all, x_send, x_recv, x_pass)
     gather_drain(kv_of(chip), kv_all, kv_send, kv_recv, kv_pass)
     gather_drain(mask_out.at[0], mask_all, m_send, m_recv, m_pass)
     gather_drain(stream_ref, s_all, s_send, s_recv, s_pass)
-    scatter_drain(part_one, got_one, one_send, one_recv)
-    scatter_drain(part_two, got_two, two_send, two_recv)
+    scatter_drain(part_one, got_one, one_sems)
+    scatter_drain(part_two, got_two, two_sems)
 
 
 def layer(
@@ -448,6 +481,8 @@
     dma = pltpu.SemaphoreType.DMA
     held = pl.BlockSpec(memory_space=pltpu.VMEM)
     left = pl.BlockSpec(memory_space=pl.ANY)
+    half = pltpu.VMEM((chips, rows, cols), jnp.bfloat16)
+    wide_half = pltpu.VMEM((chips, rows, cols), jnp.float32)
     exchange = pltpu.VMEM((devices, rows, cols), jnp.bfloat16)
     return pl.pallas_call(
         layer_kernel,
@@ -469,15 +504,17 @@
             pltpu.VMEM((KV_HEADS, rows, HEAD_DIM), jnp.float32),
             pltpu.VMEM((devices, rows, HEAD_DIM), jnp.float32),
             pltpu.VMEM((devices, rows * cols // HEAD_DIM, BLOCK), jnp.float32),
-            exchange,
-            exchange,
-            exchange,
-            exchange,
+            wide_half,
+            wide_half,
+            wide_half,
+            wide_half,
+            half,
+            half,
             pltpu.VMEM((rows, cols), jnp.float32),
             dma((5,)),
             dma(()),
             *([dma((chips,)), dma((devices,)), dma((chips,))] * 4),
-            *([dma((devices,))] * 4),
+            *([dma((chips,))] * 8),
         ],
         compiler_params=pltpu.CompilerParams(
             collective_id=0, has_side_effects=True, vmem_limit_bytes=67043328

time: 58 us -> 59.5 us (1.026)
  Pallas kernels: 54.9 us -> 56.5 us
    pallas_call x1, Pallas kernels: 54.9 us -> 56.5 us  [layer(): pl.pallas_call(layer_kernel, name='layer', out_shape=jax.ShapeDtypeStruct...]
where the time goes in v1:
time: 59.5 us; the launch traced here: 59.1 us
  Pallas kernels  56.5 us (95%)
  local copies, waits for them, and re-layouts  2.68 us (5%)
    pallas_call x1, Pallas kernels, layer(): pl.pallas_call(layer_kernel, name='layer', out_shape=jax.ShapeDtypeStruct...  56.5 us
    squeeze x1, local copies, waits for them, and re-layouts, layer(): block_mask[:, :, 0]  1.35 us
    unnamed x1, local copies, waits for them, and re-layouts  1.32 us

profile of v1, /device:TPU:0, one launch (start us, length us, event | category | flops | bytes accessed | tf_op | source)
XLA Modules:
  0.0 59.1 jit_solution(8727345968857446858)
XLA Ops:
  0.0 1.4 %copy.11.mask_ref = s32[16,8]{1,0:T(8,128)} copy(s32[16,8]{0,1:T(8,128)} %bitcast.1) | data formatting | bytes 1024 | tf_op jit(solution)/shard_map/squeeze | solution.py:532
  1.4 56.5 %layer.1 = bf16[16,512]{1,0:T(8,128)(2,1)} custom-call(bf16[16,512]{1,0:T(8,128)(2,1)} %x_ref.1, bf16[8192]{0:T(1024)(128)(2,1)} %attn_gain.1, bf16[8192,512]{1,0:T(8,128)(2,1)} %q_hbm.1, bf16[512,8192]{1,0:T(8,128)(2,1)} %o_hbm.1, bf16[8192]{0:T(1024)(128)(2,1)} %mlp_gain.1, bf16[8192,896]{1,0:T(8,128)(2,1)} %gate_hbm.1, bf16[8192,896]{1,0:T(8,128)(2,1)} %up_hbm.1, ...), custom_call_target="tpu_custom_call" | custom-call | tf_op jit(solution)/shard_map/layer/pallas_call | solution.py:487
  57.8 1.3 %copy.13 = bf16[16,512]{1,0:T(8,128)(2,1)} copy(bf16[16,512]{1,0:T(8,128)(2,1)} %layer.1) | data formatting | bytes 32768

commit v2 on v1

--- a/solution.py
+++ b/solution.py
@@ -243,14 +243,18 @@
             device_id={"seq": (me + off) % devices},
             device_id_type=pl.DeviceIdType.MESH,
         )
+    span = kv_hbm.shape[1]
+    stage = [
+        pltpu.make_async_copy(
+            kv_hbm.at[k],
+            down_w.at[k * span : (k + 1) * span, : KV_HEADS * HEAD_DIM],
+            kv_own_sem.at[k],
+        )
+        for k in range(2)
+    ]
+    for copy in stage:
+        copy.start()
     fetch_q.start()
-    own_kv = pltpu.make_async_copy(
-        kv_hbm.at[:, :, pl.ds(pl.multiple_of(chip * HEAD_DIM, HEAD_DIM), HEAD_DIM)],
-        kv_all.at[me],
-        kv_own_sem,
-    )
-    own_kv.start()
-    fetch_o.start()
     for g in range(KV_HEADS):
         mask_out[g] = jnp.broadcast_to(
             mask_ref[:, g : g + 1].astype(jnp.float32), (rows, HEAD_DIM)
@@ -262,7 +266,13 @@
     gather_start(x_ref, x_all, x_send, x_recv)
 
     def kv_of(where):
-        return kv_hbm.at[:, :, pl.ds(pl.multiple_of(where * HEAD_DIM, HEAD_DIM), HEAD_DIM)]
+        at = pl.ds(pl.multiple_of(where * HEAD_DIM, HEAD_DIM), HEAD_DIM)
+        return down_w.at[: 2 * span, at]
+
+    for copy in stage:
+        copy.wait()
+    own_kv = pltpu.make_async_copy(kv_of(chip), kv_all.at[me], kv_own_sem.at[2])
+    own_kv.start()
 
     for off in FAR_FIRST:
         there = chip_at(off)
@@ -271,9 +281,6 @@
         remote(mask_out.at[there], mask_all.at[me], m_send.at[off], m_recv.at[me], to).start()
     remote(kv_of(chip), kv_all.at[me], kv_send.at[0], kv_recv.at[me], partner).start()
     remote(mask_out.at[chip], mask_all.at[me], m_send.at[0], m_recv.at[me], partner).start()
-    fetch_gate.start()
-    fetch_up.start()
-    fetch_down.start()
 
     def norm(values, gain):
         squares = jnp.zeros((rows, cols), jnp.float32)
@@ -288,6 +295,7 @@
 
     gather_pass(x_all, x_send, x_recv, x_pass)
     gather_finish(x_all, x_send, x_recv)
+    fetch_o.start()
     norm(x_all, attn_gain)
     fetch_q.wait()
     step = 4
@@ -311,6 +319,8 @@
 
     gather_pass(kv_all, kv_send, kv_recv, kv_pass)
     gather_pass(mask_all, m_send, m_recv, m_pass)
+    fetch_gate.start()
+    fetch_up.start()
     own_kv.wait()
     gather_finish(kv_all, kv_send, kv_recv)
     gather_finish(mask_all, m_send, m_recv)
@@ -323,7 +333,7 @@
         score = (
             lax.dot_general(
                 query,
-                kv_all[c, 0],
+                kv_all[c, :span],
                 (((1,), (1,)), ((), ())),
                 preferred_element_type=jnp.float32,
             )
@@ -340,7 +350,7 @@
         factor = jnp.exp(tops[c] - top)
         total = total + factor * jnp.sum(weight, axis=-1, keepdims=True)
         accum = accum + factor * jnp.dot(
-            weight.astype(jnp.bfloat16), kv_all[c, 1], preferred_element_type=jnp.float32
+            weight.astype(jnp.bfloat16), kv_all[c, span:], preferred_element_type=jnp.float32
         )
     ratio = accum / total
     attended = jnp.concatenate(
@@ -425,6 +435,8 @@
         for s in range(chips - 1):
             remote(part.at[0], got.at[chip], send.at[s], recv.at[chip], partner).wait_send()
 
+    gather_drain(kv_of(chip), kv_all, kv_send, kv_recv, kv_pass)
+    fetch_down.start()
     fetch_o.wait()
     attn_out = scatter(attended, o_w, pair_out, pair_in, part_one, got_one, one_sems)
     stream = (x_ref[...].astype(jnp.float32) + attn_out).astype(jnp.bfloat16)
@@ -455,7 +467,6 @@
     y_ref[...] = (stream_ref[...].astype(jnp.float32) + down_out).astype(jnp.bfloat16)
 
     gather_drain(x_ref, x_all, x_send, x_recv, x_pass)
-    gather_drain(kv_of(chip), kv_all, kv_send, kv_recv, kv_pass)
     gather_drain(mask_out.at[0], mask_all, m_send, m_recv, m_pass)
     gather_drain(stream_ref, s_all, s_send, s_recv, s_pass)
     scatter_drain(part_one, got_one, one_sems)
@@ -500,7 +511,7 @@
             exchange,
             exchange,
             pltpu.VMEM((rows, cols), jnp.bfloat16),
-            pltpu.VMEM((devices, 2, BLOCK, HEAD_DIM), jnp.bfloat16),
+            pltpu.VMEM((devices, 2 * BLOCK, HEAD_DIM), jnp.bfloat16),
             pltpu.VMEM((KV_HEADS, rows, HEAD_DIM), jnp.float32),
             pltpu.VMEM((devices, rows, HEAD_DIM), jnp.float32),
             pltpu.VMEM((devices, rows * cols // HEAD_DIM, BLOCK), jnp.float32),
@@ -512,7 +523,7 @@
             half,
             pltpu.VMEM((rows, cols), jnp.float32),
             dma((5,)),
-            dma(()),
+            dma((3,)),
             *([dma((chips,)), dma((devices,)), dma((chips,))] * 4),
             *([dma((chips,))] * 8),
         ],

time: 59.5 us -> 59.6 us (level)
  no operation moved by 1% of the time
where the time goes in v2:
time: 59.6 us; the launch traced here: 59.2 us
  Pallas kernels  56.5 us (95%)
  local copies, waits for them, and re-layouts  2.68 us (4%)
    pallas_call x1, Pallas kernels, layer(): pl.pallas_call(layer_kernel, name='layer', out_shape=jax.ShapeDtypeStruct...  56.5 us
    squeeze x1, local copies, waits for them, and re-layouts, layer(): block_mask[:, :, 0]  1.35 us
    unnamed x1, local copies, waits for them, and re-layouts  1.32 us

profile of v2, /device:TPU:0, one launch (start us, length us, event | category | flops | bytes accessed | tf_op | source)
XLA Modules:
  0.0 59.2 jit_solution(7322055610737927905)
XLA Ops:
  0.0 1.4 %copy.11.mask_ref = s32[16,8]{1,0:T(8,128)} copy(s32[16,8]{0,1:T(8,128)} %bitcast.1) | data formatting | bytes 1024 | tf_op jit(solution)/shard_map/squeeze | solution.py:543
  1.4 56.5 %layer.1 = bf16[16,512]{1,0:T(8,128)(2,1)} custom-call(bf16[16,512]{1,0:T(8,128)(2,1)} %x_ref.1, bf16[8192]{0:T(1024)(128)(2,1)} %attn_gain.1, bf16[8192,512]{1,0:T(8,128)(2,1)} %q_hbm.1, bf16[512,8192]{1,0:T(8,128)(2,1)} %o_hbm.1, bf16[8192]{0:T(1024)(128)(2,1)} %mlp_gain.1, bf16[8192,896]{1,0:T(8,128)(2,1)} %gate_hbm.1, bf16[8192,896]{1,0:T(8,128)(2,1)} %up_hbm.1, ...), custom_call_target="tpu_custom_call" | custom-call | tf_op jit(solution)/shard_map/layer/pallas_call | solution.py:498
  57.8 1.3 %copy.13 = bf16[16,512]{1,0:T(8,128)(2,1)} copy(bf16[16,512]{1,0:T(8,128)(2,1)} %layer.1) | data formatting | bytes 32768

commit v3 on v1

--- a/solution.py
+++ b/solution.py
@@ -254,7 +254,7 @@
     for g in range(KV_HEADS):
         mask_out[g] = jnp.broadcast_to(
             mask_ref[:, g : g + 1].astype(jnp.float32), (rows, HEAD_DIM)
-        )
+        ).astype(jnp.bfloat16)
     mask_all[me] = mask_out[chip]
     x_all[me] = x_ref[...]
     pl.semaphore_wait(barrier, devices - 1)
@@ -316,7 +316,7 @@
     gather_finish(mask_all, m_send, m_recv)
 
     def live_at(c):
-        return jnp.concatenate([mask_all[c]] * group, axis=0) > 0.5
+        return jnp.concatenate([mask_all[c].astype(jnp.float32)] * group, axis=0) > 0.5
 
     tops = []
     for c in range(devices):
@@ -501,8 +501,8 @@
             exchange,
             pltpu.VMEM((rows, cols), jnp.bfloat16),
             pltpu.VMEM((devices, 2, BLOCK, HEAD_DIM), jnp.bfloat16),
-            pltpu.VMEM((KV_HEADS, rows, HEAD_DIM), jnp.float32),
-            pltpu.VMEM((devices, rows, HEAD_DIM), jnp.float32),
+            pltpu.VMEM((KV_HEADS, rows, HEAD_DIM), jnp.bfloat16),
+            pltpu.VMEM((devices, rows, HEAD_DIM), jnp.bfloat16),
             pltpu.VMEM((devices, rows * cols // HEAD_DIM, BLOCK), jnp.float32),
             wide_half,
             wide_half,

time: 59.5 us -> 59 us (level)
  Pallas kernels: 56.5 us -> 55.9 us
where the time goes in v3:
time: 59 us; the launch traced here: 58.6 us
  Pallas kernels  55.9 us (95%)
  local copies, waits for them, and re-layouts  2.68 us (5%)
    pallas_call x1, Pallas kernels, layer(): pl.pallas_call(layer_kernel, name='layer', out_shape=jax.ShapeDtypeStruct...  55.9 us
    squeeze x1, local copies, waits for them, and re-layouts, layer(): block_mask[:, :, 0]  1.35 us
    unnamed x1, local copies, waits for them, and re-layouts  1.32 us

profile of v3, /device:TPU:0, one launch (start us, length us, event | category | flops | bytes accessed | tf_op | source)
XLA Modules:
  0.0 58.6 jit_solution(7980444100957642388)
XLA Ops:
  0.0 1.4 %copy.11.mask_ref = s32[16,8]{1,0:T(8,128)} copy(s32[16,8]{0,1:T(8,128)} %bitcast.1) | data formatting | bytes 1024 | tf_op jit(solution)/shard_map/squeeze | solution.py:532
  1.4 55.9 %layer.1 = bf16[16,512]{1,0:T(8,128)(2,1)} custom-call(bf16[16,512]{1,0:T(8,128)(2,1)} %x_ref.1, bf16[8192]{0:T(1024)(128)(2,1)} %attn_gain.1, bf16[8192,512]{1,0:T(8,128)(2,1)} %q_hbm.1, bf16[512,8192]{1,0:T(8,128)(2,1)} %o_hbm.1, bf16[8192]{0:T(1024)(128)(2,1)} %mlp_gain.1, bf16[8192,896]{1,0:T(8,128)(2,1)} %gate_hbm.1, bf16[8192,896]{1,0:T(8,128)(2,1)} %up_hbm.1, ...), custom_call_target="tpu_custom_call" | custom-call | tf_op jit(solution)/shard_map/layer/pallas_call | solution.py:487
  57.3 1.3 %copy.13 = bf16[16,512]{1,0:T(8,128)(2,1)} copy(bf16[16,512]{1,0:T(8,128)(2,1)} %layer.1) | data formatting | bytes 32768
